TPU v7x, 256 devices: a whole 4x4x8 slice. The times are simulated.
256 devices in a mesh: view: 32 (over z, y_lo, core), head: 8 (over x, y_hi).
Axes of the slice: x: 4, y: 4 (y_hi: 2, y_lo: 2; y = y_hi * 2 + y_lo), z: 8, core: 2. Of those that a mesh axis runs over, the one named last changes fastest.
Arguments:
- tokens: bfloat16 [8192, 1536], P('view'), may hold values from -8 to 8
- timesteps: int32 [128], P('view'), may hold values from 0 to 999
- adjacency: int32 [128, 6], P('view'), may hold values from 0 to 127, as said below
- neighbour_count: int32 [128], P('view'), may hold values from 2 to 6, as said below
- anchor: int32 [1], replicated, may hold values from 0 to 127
- mod_weight: bfloat16 [256, 6, 1536], P(None, None, 'head'), may hold values from -1.5 to 1.5
- qkv_weight: bfloat16 [1536, 3, 1536], P(None, None, 'head'), may hold values from -1 to 1
- qk_gain: float32 [2, 1536], P(None, 'head'), may hold values from 0.6 to 7.2
- out_weight: bfloat16 [1536, 1536], P('head'), may hold values from -0.15625 to 0.15625
- up_weight: bfloat16 [1536, 6144], P(None, 'head'), may hold values from -0.15625 to 0.15625
- down_weight: bfloat16 [6144, 1536], P('head'), may hold values from -0.078125 to 0.078125
Outputs:
- output: bfloat16 [8192, 1536], P('view')
Inputs may be any that keep to these rules, and one draw needn't show every extreme that they name: `adjacency`: views lie on a closed camera orbit of 128 views (view 128 - 1 beside view 0). Row v names 6 different views other than v, each at most 8 views from v along the orbit; in every draw some used neighbour is exactly 8 views away on each side. Only the first neighbour_count[v] entries are used. `neighbour_count`: some view has 6 neighbours and some view has 2 in every draw.
All inputs are finite; a program needn't handle non-finite values.
Results may differ from a plain program's by a relative error of at most 0.025.
Values may be sent and summed in bfloat16 or wider, within the bound.
A program may use at most 128 MiB of HBM per device.

v0:
```python
import math
import jax
import jax.numpy as jnp
from jax import lax
from jax.sharding import PartitionSpec as P

HD = 64
RADIUS = 8
EPSILON = 1e-06


def shifted(block, axis, distance):
    devices = range(lax.axis_size(axis))
    route = [((i - distance) % len(devices), i) for i in devices]
    return lax.ppermute(block, axis, route)


def from_root(shard, axis, root):
    mine = lax.axis_index(axis) == root
    return lax.psum(jnp.where(mine, shard, jnp.zeros_like(shard)), axis)


def layer_norm(values):
    centre = values - jnp.mean(values, axis=-1, keepdims=True)
    return centre * lax.rsqrt(jnp.mean(centre * centre, axis=-1, keepdims=True) + EPSILON)


def head_norm(values, qk_gains):
    return (
        values * lax.rsqrt(jnp.mean(values * values, axis=-1, keepdims=True) + EPSILON) * qk_gains
    )


def time_features(steps_in, freq_count):
    half_count = freq_count // 2
    frequency = jnp.exp(-math.log(10000.0) * jnp.arange(half_count, dtype=jnp.float32) / half_count)
    angles = steps_in.astype(jnp.float32)[:, None] * frequency[None, :]
    return jnp.concatenate([jnp.cos(angles), jnp.sin(angles)], axis=-1)


def body(
    tokens,
    timesteps,
    adjacency,
    neighbour_count,
    anchor,
    mod_weight,
    qkv_weight,
    qk_gain,
    out_weight,
    up_weight,
    down_weight,
):
    view_count = timesteps.shape[0]
    row_count, model_width = tokens.shape
    view_tokens = row_count // view_count
    local_width = qkv_weight.shape[2]
    local_heads = local_width // HD
    total_views = view_count * lax.axis_size("view")
    first_view = lax.axis_index("view") * view_count
    features = time_features(timesteps, mod_weight.shape[0])
    activated = jax.nn.silu(features).astype(jnp.bfloat16)
    mod_part = jnp.einsum("vf,fsd->vsd", activated, mod_weight, preferred_element_type=jnp.float32)
    modulation = lax.all_gather(mod_part, "head", axis=2, tiled=True)
    inputs = tokens.reshape(view_count, view_tokens, model_width).astype(jnp.float32)
    first_in = (
        layer_norm(inputs) * (1.0 + modulation[:, 1][:, None]) + modulation[:, 0][:, None]
    ).astype(jnp.bfloat16)
    projected = jnp.einsum(
        "vtd,dsc->vtsc", first_in, qkv_weight, preferred_element_type=jnp.float32
    )
    projected = projected.reshape(view_count, view_tokens, 3, local_heads, HD)
    qk_gains = qk_gain.reshape(2, local_heads, HD)
    queries = head_norm(projected[:, :, 0], qk_gains[0]).astype(jnp.bfloat16)
    keys_here = head_norm(projected[:, :, 1], qk_gains[1]).astype(jnp.bfloat16)
    values_here = projected[:, :, 2].astype(jnp.bfloat16)
    kv_block = jnp.concatenate(
        [
            keys_here.reshape(view_count, view_tokens, local_width),
            values_here.reshape(view_count, view_tokens, local_width),
        ],
        axis=-1,
    )
    reach = RADIUS // view_count
    distances = list(range(reach, 0, -1)) + list(range(-1, -reach - 1, -1))
    fetched = [shifted(kv_block, "view", distance) for distance in distances]
    lower_blocks = fetched[:reach]
    upper_blocks = fetched[reach:]
    candidates = jnp.concatenate(lower_blocks + [kv_block] + upper_blocks, axis=0)
    anchor_view = anchor[0]
    owner_index = anchor_view // view_count
    own_piece = lax.dynamic_index_in_dim(kv_block, anchor_view % view_count, 0, keepdims=False)
    anchor_block = from_root(own_piece, "view", owner_index)
    local_ids = jnp.arange(view_count, dtype=jnp.int32)
    global_ids = first_view + local_ids
    half_views = total_views // 2
    offsets = (adjacency - global_ids[:, None] + half_views) % total_views - half_views
    slot_ids = jnp.concatenate(
        [(RADIUS + local_ids)[:, None], RADIUS + local_ids[:, None] + offsets], axis=1
    )
    chosen = candidates[slot_ids]
    anchor_rows = jnp.broadcast_to(anchor_block[None, None], (view_count, 1) + anchor_block.shape)
    gathered = jnp.concatenate([chosen, anchor_rows], axis=1)
    block_count = gathered.shape[1]
    key_blocks = gathered[..., :local_width].reshape(
        view_count, block_count, view_tokens, local_heads, HD
    )
    value_blocks = gathered[..., local_width:].reshape(
        view_count, block_count, view_tokens, local_heads, HD
    )
    usable = jnp.concatenate(
        [
            jnp.ones((view_count, 1), dtype=bool),
            jnp.arange(adjacency.shape[1], dtype=jnp.int32)[None, :] < neighbour_count[:, None],
            jnp.ones((view_count, 1), dtype=bool),
        ],
        axis=1,
    )
    scores = jnp.einsum(
        "vthe,vbshe->vhtbs", queries, key_blocks, preferred_element_type=jnp.float32
    ) * (1.0 / math.sqrt(HD))
    scores = jnp.where(usable[:, None, None, :, None], scores, -jnp.inf)
    largest = jnp.max(scores, axis=(3, 4), keepdims=True)
    powers = jnp.exp(scores - largest)
    weights = (powers / jnp.sum(powers, axis=(3, 4), keepdims=True)).astype(jnp.bfloat16)
    attended = jnp.einsum(
        "vhtbs,vbshe->vthe", weights, value_blocks, preferred_element_type=jnp.float32
    ).astype(jnp.bfloat16)
    attended = attended.reshape(row_count, local_width)
    attn_total = lax.psum(
        jnp.dot(attended, out_weight, preferred_element_type=jnp.float32).astype(jnp.bfloat16),
        "head",
    ).astype(jnp.float32)
    residual = inputs + modulation[:, 2][:, None] * attn_total.reshape(
        view_count, view_tokens, model_width
    )
    second_in = (
        layer_norm(residual) * (1.0 + modulation[:, 4][:, None]) + modulation[:, 3][:, None]
    ).astype(jnp.bfloat16)
    hidden = jax.nn.gelu(
        jnp.dot(
            second_in.reshape(row_count, model_width), up_weight, preferred_element_type=jnp.float32
        ),
        approximate=True,
    ).astype(jnp.bfloat16)
    mlp_total = lax.psum(
        jnp.dot(hidden, down_weight, preferred_element_type=jnp.float32).astype(jnp.bfloat16),
        "head",
    ).astype(jnp.float32)
    finished = residual + modulation[:, 5][:, None] * mlp_total.reshape(
        view_count, view_tokens, model_width
    )
    result = finished.astype(jnp.bfloat16).reshape(row_count, model_width)
    return result


def solution(mesh):
    return jax.shard_map(
        body,
        mesh=mesh,
        in_specs=(
            P("view", None),
            P("view"),
            P("view", None),
            P("view"),
            P(),
            P(None, None, "head"),
            P(None, None, "head"),
            P(None, "head"),
            P("head", None),
            P(None, "head"),
            P("head", None),
        ),
        out_specs=P("view", None),
        check_vma=False,
    )
```

profile of v0, /device:TPU:32, one launch (start us, length us, event | category | flops | bytes accessed | tf_op | source)
XLA Modules:
  0.0 453.6 jit_solution(16673640462495064002)
XLA Ops:
  7.5 1.3 fusion.51
  9.0 70.6 %all_gather.3 = f32[4,6,1536]{1,0,2:T(4,128)S(1)} all-gather(f32[4,6,192]{1,0,2:T(4,128)S(1)} %copy.47), channel_id=1, replica_groups=mesh['view'=32,'head'=8] {'head'}, dimensions={2}, use_global_device_ids=true | all-gather | bytes 165888 | tf_op jit(solution)/shard_map/all_gather | solution.py:64
  79.6 11.9 %fusion.62 = (f32[4,1,1536]{1,0,2:T(4,128)}, f32[4,1,1536]{1,0,2:T(4,128)}, f32[4,1,1536]{1,0,2:T(4,128)}, f32[4,1,1536]{1,0,2:T(4,128)}, f32[4,1,1536]{1,0,2:T(4,128)}, /*index=5*/f32[4,1,1536]{1,0,2:T(4,128)}) fusion(f32[4,6,1536]{1,0,2:T(4,128)S(1)} %all_gather.3), kind=kLoop, calls=%fused_computation.110 | loop fusion | bytes 294912 | tf_op jit(solution)/shard_map/slice | solution.py:150
  91.5 3.1 copy.50
  94.6 3.2 copy.64
  99.3 1.1 fusion.65
  102.4 2.7 collective-permute-start.2
  105.0 2.0 collective-permute-start.3
  108.7 1.1 multiply_reduce_fusion.1
  114.5 1.2 pad_add_fusion
  116.4 105.4 %psum.21 = bf16[64,384]{0,1:T(8,128)(2,1)} all-reduce(bf16[64,384]{0,1:T(8,128)(2,1)} %fusion.45), channel_id=1, replica_groups=mesh['view'=32,'head'=8] {'view'}, use_global_device_ids=true, to_apply=%region_3.4 | all-reduce | flops 24576 | bytes 98304 | tf_op jit(solution)/shard_map/psum | solution.py:20
  221.9 1.8 constant_dynamic-update-slice_fusion.4
  223.7 1.8 constant_dynamic-update-slice_fusion.3
  226.3 1.8 constant_dynamic-update-slice_fusion.1
  228.1 1.8 constant_dynamic-update-slice_fusion
  229.9 4.0 gather_fusion
  234.0 4.4 fusion.8
  238.3 2.6 copy.53
  240.9 2.1 fusion
  243.1 0.8 fusion.1
  244.5 1.1 fusion.21
  245.9 2.3 convolution_convert_fusion.1
  248.4 3.1 copy.59
  251.5 3.1 copy.65
  254.6 3.1 copy.48
  257.7 88.3 %all-reduce.3.cloned.1.call-done = bf16[256,1536]{1,0:T(8,128)(2,1)} async-done(((bf16[256,1536]{1,0:T(8,128)(2,1)}), bf16[256,1536]{1,0:T(8,128)(2,1)}) %all-reduce.3.cloned.1.call-update) | async-done | bytes 786448 | tf_op jit(solution)/shard_map/psum | solution.py:130
  346.0 1.5 fusion.24
  348.0 1.4 fusion.9
  349.4 4.5 %convolution_convert_fusion = bf16[256,1536]{1,0:T(8,128)(2,1)} fusion(bf16[768,1536]{1,0:T(8,128)(2,1)S(1)} %copy-done, bf16[256,1536]{1,0:T(8,128)(2,1)} %fusion.9, bf16[1536,768]{1,0:T(8,128)(2,1)} %param.20), kind=kOutput, calls=%fused_computation.7 | convolution fusion | flops 1210122240 | bytes 6291456 | tf_op jit(solution)/shard_map/dot_general | solution.py:147
  354.0 3.1 copy.57
  357.1 87.0 %all-reduce.5.cloned.1.call-done = bf16[256,1536]{1,0:T(8,128)(2,1)} async-done(((bf16[256,1536]{1,0:T(8,128)(2,1)}), bf16[256,1536]{1,0:T(8,128)(2,1)}) %all-reduce.5.cloned.1.call-update) | async-done | bytes 786448 | tf_op jit(solution)/shard_map/psum | solution.py:146
  444.1 2.6 fusion.11
  (69 shorter events, 13.4 us)
Async XLA Ops:
  6.5 342.9 %copy-start = (bf16[768,1536]{1,0:T(8,128)(2,1)S(1)}, bf16[768,1536]{1,0:T(8,128)(2,1)}, u32[]{:S(2)}) copy-start(bf16[768,1536]{1,0:T(8,128)(2,1)} %param.21) | copy-start | bytes 7077892
  6.5 339.5 %all-reduce.3.cloned.1.call-start = ((), (), s32[]{:S(2)}) async-start(), calls=%async_computation | async-start | bytes 1572864 | tf_op jit(solution)/shard_map/psum | solution.py:130
  94.6 3.2 copy-start.1
  97.8 1.5 copy-start.9
  99.3 1.2 copy-start.6
  100.4 1.0 copy-start.3
  100.4 9.4 %copy-start.10 = (s32[4]{0:T(128)S(1)}, s32[4]{0:T(128)}, u32[]{:S(2)}) copy-start(s32[4]{0:T(128)} %param.14) | copy-start | bytes 52
  100.4 11.3 %copy-start.7 = (s32[4,6]{1,0:T(4,128)S(1)}, s32[4,6]{1,0:T(4,128)}, u32[]{:S(2)}) copy-start(s32[4,6]{1,0:T(4,128)} %param.13) | copy-start | bytes 292
  102.3 119.5 %collective-permute-start = (bf16[4,64,384]{1,2,0:T(8,128)(2,1)}, bf16[4,64,384]{1,2,0:T(8,128)(2,1)}, u32[]{:S(2)}, u32[]{:S(2)}) collective-permute-start(bf16[4,64,384]{1,2,0:T(8,128)(2,1)} %pad_maximum_fusion.1), channel_id=1, source_target_pairs={{240,0},{248,8},{0,16},{8,24},{16,32},{24,40},{32,48},{40,56},{48,... | collective-permute-start | bytes 589832 | tf_op jit(solution)/shard_map/ppermute | solution.py:15
  102.4 121.3 %collective-permute-start.1 = (bf16[4,64,384]{1,2,0:T(8,128)(2,1)}, bf16[4,64,384]{1,2,0:T(8,128)(2,1)}, u32[]{:S(2)}, u32[]{:S(2)}) collective-permute-start(bf16[4,64,384]{1,2,0:T(8,128)(2,1)} %pad_maximum_fusion.1), channel_id=1, source_target_pairs={{248,0},{0,8},{8,16},{16,24},{24,32},{32,40},{40,48},{48,56},{56,6... | collective-permute-start | bytes 589832 | tf_op jit(solution)/shard_map/ppermute | solution.py:15
  102.4 123.9 %collective-permute-start.2 = (bf16[4,64,384]{1,2,0:T(8,128)(2,1)}, bf16[4,64,384]{1,2,0:T(8,128)(2,1)}, u32[]{:S(2)}, u32[]{:S(2)}) collective-permute-start(bf16[4,64,384]{1,2,0:T(8,128)(2,1)} %pad_maximum_fusion.1), channel_id=1, source_target_pairs={{8,0},{16,8},{24,16},{32,24},{40,32},{48,40},{56,48},{64,56},{72,6... | collective-permute-start | bytes 589832 | tf_op jit(solution)/shard_map/ppermute | solution.py:15
  105.0 123.0 %collective-permute-start.3 = (bf16[4,64,384]{1,2,0:T(8,128)(2,1)}, bf16[4,64,384]{1,2,0:T(8,128)(2,1)}, u32[]{:S(2)}, u32[]{:S(2)}) collective-permute-start(bf16[4,64,384]{1,2,0:T(8,128)(2,1)} %pad_maximum_fusion.1), channel_id=1, source_target_pairs={{16,0},{24,8},{32,16},{40,24},{48,32},{56,40},{64,48},{72,56},{80,... | collective-permute-start | bytes 589832 | tf_op jit(solution)/shard_map/ppermute | solution.py:15
  228.1 5.8 %copy-start.5 = (bf16[64,384]{0,1:T(8,128)(2,1)S(1)}, bf16[64,384]{0,1:T(8,128)(2,1)}, u32[]{:S(2)}) copy-start(bf16[64,384]{0,1:T(8,128)(2,1)} %psum.21) | copy-start | bytes 147460
  238.3 2.6 copy-start.8
  243.1 1.4 copy-start.4
  248.3 195.8 %all-reduce.5.cloned.1.call-start = ((), (), s32[]{:S(2)}) async-start(), calls=%async_computation.1 | async-start | bytes 1572864 | tf_op jit(solution)/shard_map/psum | solution.py:146
  346.0 1.6 copy-start.2
Sparse Core Ops, SparseCore 0:
  248.4 97.5 all-reduce.2
  354.1 89.9 all-reduce.4
where the time goes:
time: 455 us; the launch traced here: 454 us
  blocking collectives  176 us (39%)
  waiting for transfers between devices  175 us (38%)
  local copies, waits for them, and re-layouts  49.1 us (11%)
  other arithmetic  21.6 us (5%)
  between operations  14.3 us (3%)
  matrix products  12.5 us (3%)
  starting transfers between devices  4.71 us (1%)
    psum x1, blocking collectives, from_root(): return lax.psum(jnp.where(mine, shard, jnp.zeros_like(shard)), axis)  105 us
    psum x1, waiting for transfers between devices, body(): lax.psum(jnp.dot(attended, out_weight, preferred_element_type=jnp.float32...  88.3 us
    psum x1, waiting for transfers between devices, body(): lax.psum(jnp.dot(hidden, down_weight, preferred_element_type=jnp.float32)...  87 us
    all_gather x1, blocking collectives, body(): modulation = lax.all_gather(mod_part, 'head', axis=2, tiled=True)  70.6 us
    slice x2, local copies, waits for them, and re-layouts, body(): modulation[:, 5][:, None]  15 us
    unnamed x27, local copies, waits for them, and re-layouts  12.9 us
  transfers between devices with their start and end apart: 6, of which 2 were waited for; matrix products, arithmetic and copies ran while one was open for 6% of the time, Pallas kernels for 0%

commit v1 on v0

--- a/solution.py
+++ b/solution.py
@@ -61,7 +61,9 @@
     features = time_features(timesteps, mod_weight.shape[0])
     activated = jax.nn.silu(features).astype(jnp.bfloat16)
     mod_part = jnp.einsum("vf,fsd->vsd", activated, mod_weight, preferred_element_type=jnp.float32)
-    modulation = lax.all_gather(mod_part, "head", axis=2, tiled=True)
+    modulation = jnp.concatenate(
+        lax.all_to_all(jnp.stack([mod_part] * lax.axis_size("head")), "head", 0, 0), axis=2
+    )
     inputs = tokens.reshape(view_count, view_tokens, model_width).astype(jnp.float32)
     first_in = (
         layer_norm(inputs) * (1.0 + modulation[:, 1][:, None]) + modulation[:, 0][:, None]

time: 455 us -> 380 us (0.84)
  blocking collectives: 176 us -> 119 us
  local copies, waits for them, and re-layouts: 49.1 us -> 17.8 us
  waiting for transfers between devices: 175 us -> 188 us
  starting transfers between devices: 4.71 us -> 9.72 us
    all_gather x1 -> x0, blocking collectives: 70.6 us -> none  [body(): modulation = lax.all_gather(mod_part, 'head', axis=2, tiled=True)]
    slice x5 -> x0, local copies, waits for them, and re-layouts: 24.4 us -> none  [the longest x2 15 us: body(): modulation[:, 5][:, None]]
    psum x1, blocking collectives: 105 us -> 119 us  [from_root(): return lax.psum(jnp.where(mine, shard, jnp.zeros_like(shard)), axis)]
    all_to_all x0 -> x1, starting transfers between devices: none -> 6.93 us  [body(): lax.all_to_all(jnp.stack([mod_part] * lax.axis_size('head')), 'head', 0, 0)]
    unnamed x27 -> x33, local copies, waits for them, and re-layouts: 12.9 us -> 7.2 us
    psum x1, waiting for transfers between devices: 88.3 us -> 93.8 us  [body(): lax.psum(jnp.dot(attended, out_weight, preferred_element_type=jnp.float32...]
  transfers between devices with their start and end apart: 6 -> 7, of which waited for: 2 -> 3; matrix products, arithmetic and copies ran while one was open for 6% -> 3% of each run, Pallas kernels for 0% -> 0%
where the time goes in v1:
time: 380 us; the launch traced here: 379 us
  waiting for transfers between devices  188 us (49%)
  blocking collectives  119 us (31%)
  other arithmetic  17.9 us (5%)
  local copies, waits for them, and re-layouts  17.8 us (5%)
  between operations  14.3 us (4%)
  matrix products  12.6 us (3%)
  starting transfers between devices  9.72 us (3%)
    psum x1, blocking collectives, from_root(): return lax.psum(jnp.where(mine, shard, jnp.zeros_like(shard)), axis)  119 us
    psum x1, waiting for transfers between devices, body(): lax.psum(jnp.dot(attended, out_weight, preferred_element_type=jnp.float32...  93.8 us
    psum x1, waiting for transfers between devices, body(): lax.psum(jnp.dot(hidden, down_weight, preferred_element_type=jnp.float32)...  90.1 us
  transfers between devices with their start and end apart: 7, of which 3 were waited for; matrix products, arithmetic and copies ran while one was open for 3% of the time, Pallas kernels for 0%

profile of v1, /device:TPU:32, one launch (start us, length us, event | category | flops | bytes accessed | tf_op | source)
XLA Modules:
  0.0 379.3 jit_solution(18188708349134825957)
XLA Ops:
  6.6 0.8 convert_element_type.67
  7.5 1.4 fusion.53
  8.8 0.7 stack.2
  9.6 6.9 %all-to-all-start = ((f32[8,4,6,192]{3,1,2,0:T(4,128)}), f32[8,4,6,192]{3,1,2,0:T(4,128)S(1)}, u32[]{:S(2)}, u32[]{:S(2)}) async-start(f32[8,4,6,192]{3,1,2,0:T(4,128)} %stack.2), calls=%async_computation | async-start | bytes 393216 | tf_op jit(solution)/shard_map/all_to_all | solution.py:65
  16.6 0.7 iota_compare_fusion
  18.7 0.6 pad_add_fusion
  20.2 4.5 %all-to-all-done = f32[8,4,6,192]{3,1,2,0:T(4,128)S(1)} async-done(((f32[8,4,6,192]{3,1,2,0:T(4,128)}), f32[8,4,6,192]{3,1,2,0:T(4,128)S(1)}, u32[]{:S(2)}, u32[]{:S(2)}) %all-to-all-start) | async-done | bytes 147488 | tf_op jit(solution)/shard_map/all_to_all | solution.py:65
  24.9 0.6 slice_bitcast_fusion.2
  26.4 1.1 fusion.66
  27.7 0.8 copy-done.3
  28.6 0.8 pad_maximum_fusion.1
  30.2 1.8 collective-permute-start
  32.0 0.7 fusion.45
  32.6 118.6 %psum.21 = bf16[64,384]{0,1:T(8,128)(2,1)} all-reduce(bf16[64,384]{0,1:T(8,128)(2,1)} %fusion.45), channel_id=1, replica_groups=mesh['view'=32,'head'=8] {'view'}, use_global_device_ids=true, to_apply=%region_3.4 | all-reduce | flops 24576 | bytes 98304 | tf_op jit(solution)/shard_map/psum | solution.py:20
  151.2 1.8 constant_dynamic-update-slice_fusion.4
  153.0 1.8 constant_dynamic-update-slice_fusion.3
  154.8 0.8 constant_dynamic-update-slice_fusion.2
  155.6 1.8 constant_dynamic-update-slice_fusion.1
  157.4 1.8 constant_dynamic-update-slice_fusion
  159.1 4.1 %gather_fusion = bf16[28,64,384]{1,2,0:T(8,128)(2,1)} fusion(bf16[20,64,384]{1,2,0:T(8,128)(2,1)} %constant_dynamic-update-slice_fusion, s32[1024]{0:T(1024)S(1)} %pad_clamp_fusion), kind=kCustom, calls=%fused_computation | custom fusion | bytes 2752624 | tf_op jit(solution)/shard_map/gather | solution.py:103
  163.3 4.4 %fusion.8 = (bf16[4,8,64,192]{2,3,1,0:T(8,128)(2,1)}, bf16[4,8,64,192]{2,3,1,0:T(8,128)(2,1)}) fusion(bf16[4,7,64,384]{2,3,1,0:T(8,128)(2,1)} %bitcast.134, bf16[4,1,64,384]{2,3,1,0:T(8,128)(2,1)S(1)} %broadcast_in_dim.13), kind=kLoop, calls=%fused_computation.19 | loop fusion | flops 3145728 | bytes 3145728 | tf_op jit(solution)/shard_map/concatenate | solution.py:105
  167.7 2.6 copy.30
  170.3 2.1 fusion
  172.4 0.8 fusion.1
  173.8 1.1 fusion.21
  175.3 2.3 convolution_convert_fusion.1
  177.9 93.8 %all-reduce.3.cloned.1.call-done = bf16[256,1536]{1,0:T(8,128)(2,1)} async-done(((bf16[256,1536]{1,0:T(8,128)(2,1)}), bf16[256,1536]{1,0:T(8,128)(2,1)}) %all-reduce.3.cloned.1.call-update) | async-done | bytes 786448 | tf_op jit(solution)/shard_map/psum | solution.py:132
  271.7 1.5 fusion.24
  273.8 1.4 fusion.9
  275.2 4.6 %convolution_convert_fusion = bf16[256,1536]{1,0:T(8,128)(2,1)} fusion(bf16[768,1536]{1,0:T(8,128)(2,1)S(1)} %copy-done, bf16[256,1536]{1,0:T(8,128)(2,1)} %fusion.9, bf16[1536,768]{1,0:T(8,128)(2,1)} %param.20), kind=kOutput, calls=%fused_computation.7 | convolution fusion | flops 1210122240 | bytes 6291456 | tf_op jit(solution)/shard_map/dot_general | solution.py:149
  279.8 90.1 %all-reduce.5.cloned.1.call-done = bf16[256,1536]{1,0:T(8,128)(2,1)} async-done(((bf16[256,1536]{1,0:T(8,128)(2,1)}), bf16[256,1536]{1,0:T(8,128)(2,1)}) %all-reduce.5.cloned.1.call-update) | async-done | bytes 786448 | tf_op jit(solution)/shard_map/psum | solution.py:148
  369.8 2.6 fusion.11
  (72 shorter events, 5.5 us)
Async XLA Ops:
  6.5 268.6 %copy-start = (bf16[768,1536]{1,0:T(8,128)(2,1)S(1)}, bf16[768,1536]{1,0:T(8,128)(2,1)}, u32[]{:S(2)}) copy-start(bf16[768,1536]{1,0:T(8,128)(2,1)} %param.21) | copy-start | bytes 7077892
  6.5 10.8 %copy-start.1 = (bf16[256,1536]{1,0:T(8,128)(2,1)S(1)}, bf16[256,1536]{1,0:T(8,128)(2,1)}, u32[]{:S(2)}) copy-start(bf16[256,1536]{1,0:T(8,128)(2,1)} %param.11) | copy-start | bytes 2359300
  6.5 11.4 %copy-start.11 = (f32[2,192]{1,0:T(2,128)S(1)}, f32[2,192]{1,0:T(2,128)}, u32[]{:S(2)}) copy-start(f32[2,192]{1,0:T(2,128)} %param.18) | copy-start | bytes 4612
  6.5 12.0 %copy-start.12 = (s32[4,6]{1,0:T(4,128)S(1)}, s32[4,6]{1,0:T(4,128)}, u32[]{:S(2)}) copy-start(s32[4,6]{1,0:T(4,128)} %param.13) | copy-start | bytes 292
  9.6 15.1 %all-to-all-start = ((f32[8,4,6,192]{3,1,2,0:T(4,128)}), f32[8,4,6,192]{3,1,2,0:T(4,128)S(1)}, u32[]{:S(2)}, u32[]{:S(2)}) async-start(f32[8,4,6,192]{3,1,2,0:T(4,128)} %stack.2), calls=%async_computation | async-start | bytes 393216 | tf_op jit(solution)/shard_map/all_to_all | solution.py:65
  16.5 255.2 %all-reduce.3.cloned.1.call-start = ((), (), s32[]{:S(2)}) async-start(), calls=%async_computation.1 | async-start | bytes 1572864 | tf_op jit(solution)/shard_map/psum | solution.py:132
  24.9 1.5 copy-start.14
  27.5 1.0 copy-start.3
  27.5 1.0 copy-start.10
  29.4 127.9 %collective-permute-start.3 = (bf16[4,64,384]{1,2,0:T(8,128)(2,1)}, bf16[4,64,384]{1,2,0:T(8,128)(2,1)}, u32[]{:S(2)}, u32[]{:S(2)}) collective-permute-start(bf16[4,64,384]{1,2,0:T(8,128)(2,1)} %pad_maximum_fusion.1), channel_id=1, source_target_pairs={{16,0},{24,8},{32,16},{40,24},{48,32},{56,40},{64,48},{72,56},{80,... | collective-permute-start | bytes 589832 | tf_op jit(solution)/shard_map/ppermute | solution.py:15
  29.7 125.9 %collective-permute-start.2 = (bf16[4,64,384]{1,2,0:T(8,128)(2,1)}, bf16[4,64,384]{1,2,0:T(8,128)(2,1)}, u32[]{:S(2)}, u32[]{:S(2)}) collective-permute-start(bf16[4,64,384]{1,2,0:T(8,128)(2,1)} %pad_maximum_fusion.1), channel_id=1, source_target_pairs={{8,0},{16,8},{24,16},{32,24},{40,32},{48,40},{56,48},{64,56},{72,6... | collective-permute-start | bytes 589832 | tf_op jit(solution)/shard_map/ppermute | solution.py:15
  29.7 123.3 %collective-permute-start.1 = (bf16[4,64,384]{1,2,0:T(8,128)(2,1)}, bf16[4,64,384]{1,2,0:T(8,128)(2,1)}, u32[]{:S(2)}, u32[]{:S(2)}) collective-permute-start(bf16[4,64,384]{1,2,0:T(8,128)(2,1)} %pad_maximum_fusion.1), channel_id=1, source_target_pairs={{248,0},{0,8},{8,16},{16,24},{24,32},{32,40},{40,48},{48,56},{56,6... | collective-permute-start | bytes 589832 | tf_op jit(solution)/shard_map/ppermute | solution.py:15
  30.2 121.0 %collective-permute-start = (bf16[4,64,384]{1,2,0:T(8,128)(2,1)}, bf16[4,64,384]{1,2,0:T(8,128)(2,1)}, u32[]{:S(2)}, u32[]{:S(2)}) collective-permute-start(bf16[4,64,384]{1,2,0:T(8,128)(2,1)} %pad_maximum_fusion.1), channel_id=1, source_target_pairs={{240,0},{248,8},{0,16},{8,24},{16,32},{24,40},{32,48},{40,56},{48,... | collective-permute-start | bytes 589832 | tf_op jit(solution)/shard_map/ppermute | solution.py:15
  159.1 4.1 %copy-start.6 = (bf16[64,384]{0,1:T(8,128)(2,1)S(1)}, bf16[64,384]{0,1:T(8,128)(2,1)}, u32[]{:S(2)}) copy-start(bf16[64,384]{0,1:T(8,128)(2,1)} %psum.21) | copy-start | bytes 147460
  167.7 2.6 copy-start.13
  172.4 1.4 copy-start.4
  175.0 96.8 %copy-start.5 = (f32[4,1536]{1,0:T(4,128)S(1)}, f32[4,1536]{1,0:T(4,128)}, u32[]{:S(2)}) copy-start(f32[4,1536]{1,0:T(4,128)} %get-tuple-element.14) | copy-start | bytes 73732
  177.7 192.2 %all-reduce.5.cloned.1.call-start = ((), (), s32[]{:S(2)}) async-start(), calls=%async_computation.2 | async-start | bytes 1572864 | tf_op jit(solution)/shard_map/psum | solution.py:148
  271.7 1.6 copy-start.2
  271.7 2.0 copy-start.8
  271.7 2.0 copy-start.9
  275.2 94.7 %copy-start.7 = (f32[4,1536]{1,0:T(4,128)S(1)}, f32[4,1536]{1,0:T(4,128)}, u32[]{:S(2)}) copy-start(f32[4,1536]{1,0:T(4,128)} %get-tuple-element.9) | copy-start | bytes 73732
Sparse Core Ops, SparseCore 0:
  177.8 93.8 all-reduce.2
  279.9 89.9 all-reduce.4
